TPU v7x, 32 devices: a whole 2x2x4 slice. The times are simulated.
32 devices in a mesh: grp: 2 (over x), tok: 4 (over z), head: 4 (over y, core).
Axes of the slice: x: 2, y: 2, z: 4, core: 2. Of those that a mesh axis runs over, the one named last changes fastest.
Arguments:
- views: bfloat16 [2, 2, 768, 1024], P('grp', None, 'tok'), may hold values from -6 to 6
- q_weight: bfloat16 [1024, 1024], P(None, 'head'), may hold values from -0.1875 to 0.1875
- k_weight: bfloat16 [1024, 1024], P(None, 'head'), may hold values from -0.1875 to 0.1875
- v_weight: bfloat16 [1024, 1024], P(None, 'head'), may hold values from -0.1875 to 0.1875
- rate_weight: bfloat16 [1024, 4], P(None, 'head'), may hold values from -0.1875 to 0.1875
- fast_in: float32 [4, 256, 1024], P('head', None, 'tok'), may hold values from -0.375 to 0.375
- fast_out: float32 [4, 512, 256], P('head', None, 'tok'), may hold values from -0.25 to 0.25
- out_gain: float32 [1024], P('head'), may hold values from 0.1 to 1.9
Outputs:
- rendered: bfloat16 [2, 2, 768, 1024], P('grp', None, 'tok', 'head')
All inputs are finite; a program needn't handle non-finite values.
Results may differ from a plain program's by a relative error of at most 0.013.
Values may be sent and summed in bfloat16 or wider, within the bound.
A program may use at most 64 MiB of HBM per device.

v0:
```python
import math
import jax
import jax.numpy as jnp
from jax import lax
from jax.sharding import PartitionSpec as P

norm_eps = 1e-06
out_eps = 1e-05
step_coef = 0.3
momentum_keep = 0.5


def spread(value, axis, source):
    kept = jnp.where(lax.axis_index(axis) == source, value, 0).astype(value.dtype)
    return lax.psum(kept, axis)


def rms_scale(values):
    return values * lax.rsqrt(jnp.mean(values * values, axis=-1, keepdims=True) + norm_eps)


def contract_rows(left, right):
    return lax.dot_general(
        left, right, (((0,), (0,)), ((), ())), preferred_element_type=jnp.float32
    )


def contract_cols(left, right):
    return lax.dot_general(
        left, right, (((1,), (1,)), ((), ())), preferred_element_type=jnp.float32
    )


def fast_apply(queries, copy_in, copy_out):
    hidden_units = copy_out.shape[0]
    pre_act = jnp.dot(queries, copy_in, preferred_element_type=jnp.float32)
    gate = pre_act[:, :hidden_units]
    upper = pre_act[:, hidden_units:]
    hidden = (gate * jax.nn.sigmoid(gate) * upper).astype(jnp.bfloat16)
    return jnp.dot(hidden, copy_out, preferred_element_type=jnp.float32)


def local(views, q_weight, k_weight, v_weight, rate_weight, fast_in, fast_out, out_gain):
    tok_count = lax.axis_size("tok")
    is_input = lax.axis_index("grp") == 0
    spans = views.shape[1]
    head_size = fast_in.shape[1]
    hidden_units = fast_out.shape[1]
    step_size = step_coef / math.sqrt(views.shape[2] * tok_count)
    width_all = head_size * lax.axis_size("head")
    whole_in, whole_out = (
        lax.all_gather(fast_in, "tok", axis=2, tiled=True),
        lax.all_gather(fast_out, "tok", axis=2, tiled=True),
    )
    whole_in = whole_in[0]
    whole_out = whole_out[0]
    copy_in = whole_in.astype(jnp.bfloat16)
    copy_out = whole_out.astype(jnp.bfloat16)
    state_in = fast_in[0]
    state_out = fast_out[0]
    base_in = jnp.mean(state_in * state_in, axis=0, keepdims=True)
    base_out = jnp.mean(state_out * state_out, axis=0, keepdims=True)
    moment_in = jnp.zeros_like(state_in)
    moment_out = jnp.zeros_like(state_out)

    def input_grads(inputs, given_in, given_out):
        keyed = rms_scale(jnp.dot(inputs, k_weight, preferred_element_type=jnp.float32)).astype(
            jnp.bfloat16
        )
        valued = jnp.dot(inputs, v_weight, preferred_element_type=jnp.float32)
        rates = jax.nn.softplus(jnp.dot(inputs, rate_weight, preferred_element_type=jnp.float32))
        upstream = (-(step_size * rates) * valued).astype(jnp.bfloat16)
        pre_act = jnp.dot(keyed, given_in, preferred_element_type=jnp.float32)
        gate = pre_act[:, :hidden_units]
        upper = pre_act[:, hidden_units:]
        sigma = jax.nn.sigmoid(gate)
        active = gate * sigma
        hidden = (active * upper).astype(jnp.bfloat16)
        grad_out = contract_rows(hidden, upstream)
        back = contract_cols(upstream, given_out)
        back_pre = jnp.concatenate(
            [back * upper * sigma * (1.0 + gate * (1.0 - sigma)), back * active], axis=1
        ).astype(jnp.bfloat16)
        grad_in = contract_rows(keyed, back_pre)
        return (grad_in, grad_out)

    def novel_grads(inputs, given_in, given_out):
        return (
            jnp.zeros((head_size, 2 * hidden_units), jnp.float32),
            jnp.zeros((hidden_units, head_size), jnp.float32),
        )

    outputs = []
    for span in range(spans):
        inputs = views[0, span]
        queries = rms_scale(jnp.dot(inputs, q_weight, preferred_element_type=jnp.float32)).astype(
            jnp.bfloat16
        )
        grads = lax.cond(is_input, input_grads, novel_grads, inputs, copy_in, copy_out)
        grad_in, grad_out = lax.psum_scatter(grads, "tok", scatter_dimension=1, tiled=True)
        moment_in = momentum_keep * moment_in + grad_in
        moment_out = momentum_keep * moment_out + grad_out
        trial_in = state_in - moment_in
        trial_out = state_out - moment_out
        mean_in = jnp.mean(trial_in * trial_in, axis=0, keepdims=True)
        mean_out = jnp.mean(trial_out * trial_out, axis=0, keepdims=True)
        state_in = trial_in * jnp.sqrt(base_in) * lax.rsqrt(mean_in + norm_eps)
        state_out = trial_out * jnp.sqrt(base_out) * lax.rsqrt(mean_out + norm_eps)
        part_in = state_in.astype(jnp.bfloat16)
        part_out = state_out.astype(jnp.bfloat16)
        copy_in, copy_out = (
            lax.all_gather(part_in, "tok", axis=1, tiled=True),
            lax.all_gather(part_out, "tok", axis=1, tiled=True),
        )
        copy_in, copy_out = (spread(copy_in, "grp", 0), spread(copy_out, "grp", 0))
        produced = fast_apply(queries, copy_in, copy_out)
        squares = lax.psum(jnp.sum(produced * produced, axis=1), "head")
        normed = produced * lax.rsqrt(squares / width_all + out_eps)[:, None] * out_gain
        outputs.append(normed.astype(jnp.bfloat16))
    return jnp.stack(outputs)[None]


def solution(mesh):
    placed = (
        P("grp", None, "tok", None),
        P(None, "head"),
        P(None, "head"),
        P(None, "head"),
        P(None, "head"),
        P("head", None, "tok"),
        P("head", None, "tok"),
        P("head"),
    )
    return jax.shard_map(
        local, mesh=mesh, in_specs=placed, out_specs=P("grp", None, "tok", "head"), check_vma=False
    )
```

profile of v0, /device:TPU:0, one launch (start us, length us, event | category | flops | bytes accessed | tf_op | source)
XLA Modules:
  0.0 281.3 jit_solution(5273160163596320403)
XLA Ops:
  6.5 1.2 slice_bitcast_fusion.1
  8.0 18.1 %all_gather.18 = bf16[1,512,256]{1,0,2:T(2,128)(2,1)} all-gather(bf16[1,512,64]{1,0,2:T(2,128)(2,1)S(1)} %copy.11), channel_id=1, replica_groups=mesh['grp'=2,'tok'=4,'head'=4] {'tok'}, dimensions={2}, use_global_device_ids=true | all-gather | bytes 327680 | tf_op jit(solution)/shard_map/all_gather | solution.py:53
  26.1 16.5 %all_gather.19 = bf16[1,256,1024]{2,1,0:T(8,128)(2,1)S(1)} all-gather(bf16[1,256,256]{2,1,0:T(8,128)(2,1)S(1)} %convert.16), channel_id=1, replica_groups=mesh['grp'=2,'tok'=4,'head'=4] {'tok'}, dimensions={2}, use_global_device_ids=true | all-gather | bytes 655360 | tf_op jit(solution)/shard_map/all_gather | solution.py:52
  42.6 7.0 %conditional.2 = (f32[256,1024]{1,0:T(8,128)S(1)}, f32[512,256]{1,0:T(8,128)}) conditional(s32[]{:T(128)} %convert_element_type.75, () %tuple.21, (bf16[192,1024]{1,0:T(8,128)(2,1)S(1)}, bf16[1024,256]{1,0:T(8,128)(2,1)S(1)}, bf16[1024,1]{0,1:T(2,128)(2,1)S(1)}, bf16[1024,256]{1,0:T(8,128)(2,1)S(1)}, bf16[1,512,256]{1,0,2:T(2,128)(2,1)}, ...), branch_computations={%region_1.0_spmd, %region_2.4_spmd} | conditional | flops 506758848 | bytes 14132096 | solution.py:99
  43.0 1.2 fusion.1
  44.8 0.7 copy-done.7
  45.5 0.5 copy.12
  46.0 1.4 multiply_convert_fusion.2
  47.4 0.4 fusion.4
  47.8 0.7 copy-done.11
  48.6 1.1 fusion.12
  49.7 2.4 copy.18
  52.2 0.7 reduce-scatter.9.cloned.1.call-update
  53.2 21.1 %reduce-scatter.13.cloned.1.call-done = f32[64,512]{1,0:T(8,128)} async-done(((f32[256,512]{1,0:T(8,128)}), f32[64,512]{1,0:T(8,128)}) %reduce-scatter.13.cloned.1.call-update) | async-done | bytes 131088
  74.3 1.0 copy.19
  75.6 15.5 %all_gather.21 = bf16[512,256]{0,1:T(8,128)(2,1)S(1)} all-gather(bf16[512,64]{0,1:T(8,128)(2,1)S(1)} %copy.14), channel_id=1, replica_groups=mesh['grp'=2,'tok'=4,'head'=4] {'tok'}, dimensions={1}, use_global_device_ids=true | all-gather | bytes 327680 | tf_op jit(solution)/shard_map/all_gather | solution.py:113
  91.2 0.7 broadcast_select_fusion.3
  91.9 11.3 %reduce-scatter.9.cloned.1.call-done = f32[256,256]{1,0:T(8,128)} async-done(((f32[256,1024]{1,0:T(8,128)}), f32[256,256]{1,0:T(8,128)}) %reduce-scatter.9.cloned.1.call-update) | async-done | bytes 262160 | tf_op jit(solution)/shard_map/reduce_scatter | solution.py:100
  103.2 1.1 fusion.34
  104.3 15.4 %all_gather.20 = bf16[256,1024]{1,0:T(8,128)(2,1)S(1)} all-gather(bf16[256,256]{1,0:T(8,128)(2,1)S(1)} %fusion.35), channel_id=1, replica_groups=mesh['grp'=2,'tok'=4,'head'=4] {'tok'}, dimensions={1}, use_global_device_ids=true | all-gather | bytes 655360 | tf_op jit(solution)/shard_map/all_gather | solution.py:112
  119.8 0.8 broadcast_select_fusion.1
  120.7 34.5 %all-reduce.8.cloned.1.call-done = (bf16[512,256]{0,1:T(8,128)(2,1)}, bf16[256,1024]{1,0:T(8,128)(2,1)}) async-done(((bf16[512,256]{0,1:T(8,128)(2,1)}, bf16[256,1024]{1,0:T(8,128)(2,1)}), (bf16[512,256]{0,1:T(8,128)(2,1)}, bf16[256,1024]{1,0:T(8,128)(2,1)})) %all-reduce.8.cloned.1.call-update) | async-done | bytes 786448 | tf_op jit(solution)/shard_map/psum | solution.py:15
  155.2 4.4 %conditional.3 = (f32[256,1024]{1,0:T(8,128)S(1)}, f32[512,256]{1,0:T(8,128)}) conditional(s32[]{:T(128)} %convert_element_type.75, () %tuple.23, (bf16[192,1024]{1,0:T(8,128)(2,1)S(1)}, bf16[1024,256]{1,0:T(8,128)(2,1)S(1)}, bf16[1024,1]{0,1:T(2,128)(2,1)S(1)}, bf16[1024,256]{1,0:T(8,128)(2,1)S(1)}, bf16[512,256]{0,1:T(8,128)(2,1)}, ...), branch_computations={%region_15.16_spmd, %region_16.18_spmd} | conditional | flops 506758848 | bytes 11772744 | solution.py:99
  155.6 0.7 copy-done.9
  157.1 0.7 copy-done.19
  158.0 0.4 fusion.19
  158.4 1.1 fusion.24
  159.5 2.4 copy.20
  162.0 0.5 reduce-scatter.11.cloned.1.call-update
  162.6 1.4 multiply_reduce_fusion.7
  164.0 0.4 multiply_reduce_fusion.9
  164.4 19.5 %reduce-scatter.15.cloned.1.call-done = f32[64,512]{1,0:T(8,128)} async-done(((f32[256,512]{1,0:T(8,128)}), f32[64,512]{1,0:T(8,128)}) %reduce-scatter.15.cloned.1.call-update) | async-done | bytes 131088
  184.0 1.0 copy.21
  185.2 15.6 %all_gather.23 = bf16[512,256]{0,1:T(8,128)(2,1)S(1)} all-gather(bf16[512,64]{0,1:T(8,128)(2,1)S(1)} %copy.16), channel_id=1, replica_groups=mesh['grp'=2,'tok'=4,'head'=4] {'tok'}, dimensions={1}, use_global_device_ids=true | all-gather | bytes 327680 | tf_op jit(solution)/shard_map/all_gather | solution.py:113
  200.9 0.7 broadcast_select_fusion.2
  201.6 11.1 %reduce-scatter.11.cloned.1.call-done = f32[256,256]{1,0:T(8,128)} async-done(((f32[256,1024]{1,0:T(8,128)}), f32[256,256]{1,0:T(8,128)}) %reduce-scatter.11.cloned.1.call-update) | async-done | bytes 262160 | tf_op jit(solution)/shard_map/reduce_scatter | solution.py:100
  212.7 1.0 multiply_reduce_fusion.3
  213.8 15.8 %all_gather.22 = bf16[256,1024]{1,0:T(8,128)(2,1)S(1)} all-gather(bf16[256,256]{1,0:T(8,128)(2,1)S(1)} %multiply_convert_fusion.15), channel_id=1, replica_groups=mesh['grp'=2,'tok'=4,'head'=4] {'tok'}, dimensions={1}, use_global_device_ids=true | all-gather | bytes 655360 | tf_op jit(solution)/shard_map/all_gather | solution.py:112
  229.5 0.8 broadcast_select_fusion
  230.4 1.0 copy-done.8
  231.7 0.6 copy-done.18
  232.4 0.4 multiply_reduce_fusion.8
  232.7 32.0 %all-reduce.6.cloned.1.call-done = (bf16[512,256]{0,1:T(8,128)(2,1)}, bf16[256,1024]{1,0:T(8,128)(2,1)}) async-done(((bf16[512,256]{0,1:T(8,128)(2,1)}, bf16[256,1024]{1,0:T(8,128)(2,1)}), (bf16[512,256]{0,1:T(8,128)(2,1)}, bf16[256,1024]{1,0:T(8,128)(2,1)})) %all-reduce.6.cloned.1.call-update) | async-done | bytes 786448 | tf_op jit(solution)/shard_map/psum | solution.py:15
  264.7 1.4 fusion.43
  266.1 0.4 multiply_reduce_fusion.6
  266.5 6.4 %all-reduce = (f32[192]{0:T(256)S(1)}, f32[192]{0:T(256)S(1)}) all-reduce(f32[192]{0:T(256)S(1)} %get-tuple-element.95, f32[192]{0:T(256)S(1)} %get-tuple-element.97), channel_id=1, replica_groups=mesh['grp'=2,'tok'=4,'head'=4] {'head'}, use_global_device_ids=true, to_apply=%region_25.26 | all-reduce | flops 384 | bytes 3072 | tf_op jit(solution)/shard_map/psum | solution.py:117
  272.9 0.7 copy-done.17
  273.7 0.7 maximum_bitcast_fusion
  (78 shorter events, 4.1 us)
Async XLA Ops:
  6.5 156.1 %copy-start = (bf16[1024,256]{1,0:T(8,128)(2,1)S(1)}, bf16[1024,256]{1,0:T(8,128)(2,1)}, u32[]{:S(2)}) copy-start(bf16[1024,256]{1,0:T(8,128)(2,1)} %param.13) | copy-start | bytes 1572868
  6.5 67.8 %reduce-scatter.13.cloned.1.call-start = ((), (), s32[]{:S(2)}) async-start(), calls=%async_computation.6 | async-start | bytes 655360
  6.5 1.2 copy-start.12
  7.9 18.2 %copy-start.1 = (f32[1,256,256]{2,1,0:T(8,128)S(1)}, f32[1,256,256]{2,1,0:T(8,128)}, u32[]{:S(2)}) copy-start(f32[1,256,256]{2,1,0:T(8,128)} %param.17) | copy-start | bytes 786436
  7.9 34.7 %copy-start.16 = (bf16[1024,1]{0,1:T(2,128)(2,1)S(1)}, bf16[1024,1]{0,1:T(2,128)(2,1)}, u32[]{:S(2)}) copy-start(bf16[1024,1]{0,1:T(2,128)(2,1)} %param.16) | copy-start | bytes 6148
  26.1 16.5 %copy-start.5 = (bf16[1024,256]{1,0:T(8,128)(2,1)S(1)}, bf16[1024,256]{1,0:T(8,128)(2,1)}, u32[]{:S(2)}) copy-start(bf16[1024,256]{1,0:T(8,128)(2,1)} %param.14) | copy-start | bytes 1572868
  26.1 16.5 %copy-start.6 = (bf16[1024,256]{1,0:T(8,128)(2,1)S(1)}, bf16[1024,256]{1,0:T(8,128)(2,1)}, u32[]{:S(2)}) copy-start(bf16[1024,256]{1,0:T(8,128)(2,1)} %param.15) | copy-start | bytes 1572868
  44.4 1.1 copy-start.7
  44.8 1.2 copy-start.14
  47.4 1.1 copy-start.11
  47.4 1.1 copy-start.15
  49.7 2.5 copy-start.2
  52.1 51.1 %reduce-scatter.9.cloned.1.call-start = ((), (), s32[]{:S(2)}) async-start(), calls=%async_computation.4 | async-start | bytes 1310720 | tf_op jit(solution)/shard_map/reduce_scatter | solution.py:100
  52.2 0.9 copy-start.13
  52.9 102.3 %all-reduce.8.cloned.1.call-start = ((), (), s32[]{:S(2)}) async-start(), calls=%async_computation.9 | async-start | bytes 1572864 | tf_op jit(solution)/shard_map/psum | solution.py:15
  103.2 1.1 copy-start.4
  120.6 63.3 %reduce-scatter.15.cloned.1.call-start = ((), (), s32[]{:S(2)}) async-start(), calls=%async_computation.7 | async-start | bytes 655360
  155.2 1.0 copy-start.9
  156.8 1.0 copy-start.19
  159.5 2.5 copy-start.3
  162.0 50.7 %reduce-scatter.11.cloned.1.call-start = ((), (), s32[]{:S(2)}) async-start(), calls=%async_computation.5 | async-start | bytes 1310720 | tf_op jit(solution)/shard_map/reduce_scatter | solution.py:100
  162.5 1.5 copy-start.10
  162.6 102.2 %all-reduce.6.cloned.1.call-start = ((), (), s32[]{:S(2)}) async-start(), calls=%async_computation.8 | async-start | bytes 1572864 | tf_op jit(solution)/shard_map/psum | solution.py:15
  230.4 1.0 copy-start.8
  231.4 0.9 copy-start.18
  264.7 1.4 copy-start.20
  272.9 0.7 copy-start.17
Sparse Core Ops, SparseCore 0:
  52.2 22.0 reduce-scatter.12
  76.6 26.4 reduce-scatter.8
  120.7 34.3 all-reduce.7
  162.1 21.8 reduce-scatter.14
  186.1 26.5 reduce-scatter.10
  230.5 34.1 all-reduce.5
where the time goes:
time: 282 us; the launch traced here: 281 us
  waiting for transfers between devices  131 us (46%)
  blocking collectives  103 us (37%)
  local copies, waits for them, and re-layouts  14.3 us (5%)
  between operations  13.7 us (5%)
  matrix products  12.1 us (4%)
  other arithmetic  6.49 us (2%)
    psum x2, waiting for transfers between devices, spread(): return lax.psum(kept, axis)  66.5 us
    unnamed x8, waiting for transfers between devices  42 us
    all_gather x2, blocking collectives, local(): lax.all_gather(part_in, 'tok', axis=1, tiled=True)  31.2 us
    all_gather x2, blocking collectives, local(): lax.all_gather(part_out, 'tok', axis=1, tiled=True)  31.2 us
    reduce_scatter x2, waiting for transfers between devices, local(): lax.psum_scatter(grads, 'tok', scatter_dimension=1, tiled=True)  22.4 us
    all_gather x1, blocking collectives, local(): lax.all_gather(fast_out, 'tok', axis=2, tiled=True)  18.1 us
    all_gather x1, blocking collectives, local(): lax.all_gather(fast_in, 'tok', axis=2, tiled=True)  16.5 us
    unnamed x36, local copies, waits for them, and re-layouts  9.64 us
  transfers between devices with their start and end apart: 6, of which 6 were waited for; matrix products, arithmetic and copies ran while one was open for 2% of the time, Pallas kernels for 0%

commit v1 on v0

--- a/solution.py
+++ b/solution.py
@@ -12,7 +12,7 @@
 
 def spread(value, axis, source):
     kept = jnp.where(lax.axis_index(axis) == source, value, 0).astype(value.dtype)
-    return lax.psum(kept, axis)
+    return jnp.sum(lax.all_gather(kept, axis), axis=0)
 
 
 def rms_scale(values):

time: 282 us -> 267 us (0.947)
  waiting for transfers between devices: 131 us -> 93.6 us
  blocking collectives: 103 us -> 121 us
  other arithmetic: 6.49 us -> 11.6 us
    psum x2 -> x0, waiting for transfers between devices: 66.5 us -> none  [spread(): return lax.psum(kept, axis)]
    reduce_scatter x2, waiting for transfers between devices: 22.4 us -> 53.5 us  [local(): lax.psum_scatter(grads, 'tok', scatter_dimension=1, tiled=True)]
    all_gather x0 -> x2, blocking collectives: none -> 19.8 us  [spread(): return jnp.sum(lax.all_gather(kept, axis), axis=0)]
    reduce_sum x0 -> x4, other arithmetic: none -> 6.48 us  [spread(): return jnp.sum(lax.all_gather(kept, axis), axis=0)]
  transfers between devices with their start and end apart: 6 -> 6, of which waited for: 6 -> 4; matrix products, arithmetic and copies ran while one was open for 2% -> 4% of each run, Pallas kernels for 0% -> 0%
where the time goes in v1:
time: 267 us
  blocking collectives  121 us (45%)
  waiting for transfers between devices  93.6 us (35%)
  local copies, waits for them, and re-layouts  14.9 us (6%)
  between operations  13.7 us (5%)
  matrix products  11.7 us (4%)
  other arithmetic  11.6 us (4%)
    reduce_scatter x2, waiting for transfers between devices, local(): lax.psum_scatter(grads, 'tok', scatter_dimension=1, tiled=True)  53.5 us
    unnamed x8, waiting for transfers between devices  40.1 us
    all_gather x2, blocking collectives, local(): lax.all_gather(part_in, 'tok', axis=1, tiled=True)  31.9 us
    all_gather x2, blocking collectives, local(): lax.all_gather(part_out, 'tok', axis=1, tiled=True)  28.8 us
    all_gather x2, blocking collectives, spread(): return jnp.sum(lax.all_gather(kept, axis), axis=0)  19.8 us
    all_gather x1, blocking collectives, local(): lax.all_gather(fast_out, 'tok', axis=2, tiled=True)  18.1 us
    all_gather x1, blocking collectives, local(): lax.all_gather(fast_in, 'tok', axis=2, tiled=True)  16.5 us
    unnamed x36, local copies, waits for them, and re-layouts  9.59 us
  transfers between devices with their start and end apart: 6, of which 4 were waited for; matrix products, arithmetic and copies ran while one was open for 4% of the time, Pallas kernels for 0%

profile of v1, /device:TPU:0, one launch (start us, length us, event | category | flops | bytes accessed | tf_op | source)
XLA Modules:
  0.0 266.7 jit_solution(4510759147636833709)
XLA Ops:
  6.5 1.2 slice_bitcast_fusion.1
  8.0 18.1 %all_gather.42 = bf16[1,512,256]{1,0,2:T(2,128)(2,1)} all-gather(bf16[1,512,64]{1,0,2:T(2,128)(2,1)S(1)} %copy.16), channel_id=1, replica_groups=mesh['grp'=2,'tok'=4,'head'=4] {'tok'}, dimensions={2}, use_global_device_ids=true | all-gather | bytes 327680 | tf_op jit(solution)/shard_map/all_gather | solution.py:53
  26.1 16.5 %all_gather.43 = bf16[1,256,1024]{2,1,0:T(8,128)(2,1)S(1)} all-gather(bf16[1,256,256]{2,1,0:T(8,128)(2,1)S(1)} %convert.20), channel_id=1, replica_groups=mesh['grp'=2,'tok'=4,'head'=4] {'tok'}, dimensions={2}, use_global_device_ids=true | all-gather | bytes 655360 | tf_op jit(solution)/shard_map/all_gather | solution.py:52
  42.6 7.0 %conditional.2 = (f32[256,1024]{1,0:T(8,128)S(1)}, f32[512,256]{1,0:T(8,128)}) conditional(s32[]{:T(128)} %convert_element_type.83, () %tuple.21, (bf16[192,1024]{1,0:T(8,128)(2,1)S(1)}, bf16[1024,256]{1,0:T(8,128)(2,1)S(1)}, bf16[1024,1]{0,1:T(2,128)(2,1)S(1)}, bf16[1024,256]{1,0:T(8,128)(2,1)S(1)}, bf16[1,512,256]{1,0,2:T(2,128)(2,1)}, ...), branch_computations={%region_1.0_spmd, %region_2.4_spmd} | conditional | flops 506758848 | bytes 13345608 | solution.py:99
  43.0 1.2 fusion.1
  44.8 0.7 copy-done.8
  45.5 0.5 copy.17
  46.0 1.4 multiply_convert_fusion.2
  47.4 0.4 fusion.4
  47.8 0.7 copy-done.10
  48.5 1.1 fusion.12
  49.7 2.4 copy.23
  52.2 0.7 reduce-scatter.9.cloned.1.call-update
  53.0 21.3 %reduce-scatter.13.cloned.1.call-done = f32[64,512]{1,0:T(8,128)} async-done(((f32[256,512]{1,0:T(8,128)}), f32[64,512]{1,0:T(8,128)}) %reduce-scatter.13.cloned.1.call-update) | async-done | bytes 131088
  74.3 1.0 copy.24
  75.4 26.8 %reduce-scatter.9.cloned.1.call-done = f32[256,256]{1,0:T(8,128)} async-done(((f32[256,1024]{1,0:T(8,128)}), f32[256,256]{1,0:T(8,128)}) %reduce-scatter.9.cloned.1.call-update) | async-done | bytes 262160 | tf_op jit(solution)/shard_map/reduce_scatter | solution.py:100
  102.2 1.1 fusion.34
  103.4 16.0 %all_gather.44 = bf16[256,1024]{1,0:T(8,128)(2,1)S(1)} all-gather(bf16[256,256]{1,0:T(8,128)(2,1)S(1)} %fusion.35), channel_id=1, replica_groups=mesh['grp'=2,'tok'=4,'head'=4] {'tok'}, dimensions={1}, use_global_device_ids=true | all-gather | bytes 655360 | tf_op jit(solution)/shard_map/all_gather | solution.py:112
  119.3 0.9 broadcast_select_fusion.1
  120.4 0.5 copy-done.16
  121.0 14.4 %all_gather.47 = bf16[512,256]{0,1:T(8,128)(2,1)S(1)} all-gather(bf16[512,64]{0,1:T(8,128)(2,1)S(1)} %copy.19), channel_id=1, replica_groups=mesh['grp'=2,'tok'=4,'head'=4] {'tok'}, dimensions={1}, use_global_device_ids=true | all-gather | bytes 327680 | tf_op jit(solution)/shard_map/all_gather | solution.py:113
  135.4 10.0 %all-gather.1 = bf16[1024,256]{0,1:T(8,128)(2,1)S(1)} all-gather(bf16[512,256]{0,1:T(8,128)(2,1)S(1)} %broadcast_select_fusion.3), channel_id=3, replica_groups=mesh['grp'=2,'tok'=4,'head'=4] {'grp'}, dimensions={0}, use_global_device_ids=true | all-gather | bytes 786432 | tf_op jit(solution)/shard_map/all_gather | solution.py:15
  145.4 0.4 reshape.112
  145.8 2.1 reduce_sum.162
  147.9 1.5 reduce_sum.159
  149.4 4.2 %conditional.3 = (f32[256,1024]{1,0:T(8,128)S(1)}, f32[512,256]{1,0:T(8,128)}) conditional(s32[]{:T(128)} %convert_element_type.83, () %tuple.23, (bf16[192,1024]{1,0:T(8,128)(2,1)S(1)}, bf16[1024,256]{1,0:T(8,128)(2,1)S(1)}, bf16[1024,1]{0,1:T(2,128)(2,1)S(1)}, bf16[1024,256]{1,0:T(8,128)(2,1)}, bf16[512,256]{0,1:T(8,128)(2,1)}, ...), branch_computations={%region_15.16_spmd, %region_16.18_spmd} | conditional | flops 506758848 | bytes 11772744 | solution.py:99
  150.3 0.5 copy-done.7
  151.1 0.7 copy-done.13
  152.1 0.4 fusion.19
  152.5 1.1 fusion.24
  153.6 2.4 copy.25
  156.1 0.5 reduce-scatter.11.cloned.1.call-update
  156.7 2.0 multiply_reduce_fusion.7
  159.4 0.6 copy-done.12
  160.4 17.5 %reduce-scatter.15.cloned.1.call-done = f32[64,512]{1,0:T(8,128)} async-done(((f32[256,512]{1,0:T(8,128)}), f32[64,512]{1,0:T(8,128)}) %reduce-scatter.15.cloned.1.call-update) | async-done | bytes 131088
  178.0 1.0 copy.26
  179.0 26.6 %reduce-scatter.11.cloned.1.call-done = f32[256,256]{1,0:T(8,128)} async-done(((f32[256,1024]{1,0:T(8,128)}), f32[256,256]{1,0:T(8,128)}) %reduce-scatter.11.cloned.1.call-update) | async-done | bytes 262160 | tf_op jit(solution)/shard_map/reduce_scatter | solution.py:100
  205.6 1.0 multiply_reduce_fusion.3
  206.7 16.0 %all_gather.50 = bf16[256,1024]{1,0:T(8,128)(2,1)S(1)} all-gather(bf16[256,256]{1,0:T(8,128)(2,1)S(1)} %multiply_convert_fusion.15), channel_id=1, replica_groups=mesh['grp'=2,'tok'=4,'head'=4] {'tok'}, dimensions={1}, use_global_device_ids=true | all-gather | bytes 655360 | tf_op jit(solution)/shard_map/all_gather | solution.py:112
  222.7 0.9 broadcast_select_fusion
  223.6 0.6 copy-done.17
  224.4 14.4 %all_gather.53 = bf16[512,256]{0,1:T(8,128)(2,1)S(1)} all-gather(bf16[512,64]{0,1:T(8,128)(2,1)S(1)} %copy.21), channel_id=1, replica_groups=mesh['grp'=2,'tok'=4,'head'=4] {'tok'}, dimensions={1}, use_global_device_ids=true | all-gather | bytes 327680 | tf_op jit(solution)/shard_map/all_gather | solution.py:113
  238.8 9.9 %all-gather.3 = bf16[1024,256]{0,1:T(8,128)(2,1)S(1)} all-gather(bf16[512,256]{0,1:T(8,128)(2,1)S(1)} %broadcast_select_fusion.2), channel_id=5, replica_groups=mesh['grp'=2,'tok'=4,'head'=4] {'grp'}, dimensions={0}, use_global_device_ids=true | all-gather | bytes 786432 | tf_op jit(solution)/shard_map/all_gather | solution.py:15
  249.0 1.4 reduce_sum.168
  250.5 1.5 reduce_sum.166
  252.7 5.7 %all-reduce = (f32[192]{0:T(256)S(1)}, f32[192]{0:T(256)S(1)}) all-reduce(f32[192]{0:T(256)S(1)} %get-tuple-element.97, f32[192]{0:T(256)S(1)} %get-tuple-element.99), channel_id=1, replica_groups=mesh['grp'=2,'tok'=4,'head'=4] {'head'}, use_global_device_ids=true, to_apply=%region_25.26 | all-reduce | flops 384 | bytes 3072 | tf_op jit(solution)/shard_map/psum | solution.py:117
  258.4 0.7 copy-done.18
  259.2 0.7 maximum_bitcast_fusion
  (82 shorter events, 5.8 us)
Async XLA Ops:
  6.5 150.2 %copy-start = (bf16[1024,256]{1,0:T(8,128)(2,1)S(1)}, bf16[1024,256]{1,0:T(8,128)(2,1)}, u32[]{:S(2)}) copy-start(bf16[1024,256]{1,0:T(8,128)(2,1)} %param.13) | copy-start | bytes 1572868
  6.5 67.8 %reduce-scatter.13.cloned.1.call-start = ((), (), s32[]{:S(2)}) async-start(), calls=%async_computation.8 | async-start | bytes 655360
  6.5 1.2 copy-start.11
  7.9 18.2 %copy-start.1 = (f32[1,256,256]{2,1,0:T(8,128)S(1)}, f32[1,256,256]{2,1,0:T(8,128)}, u32[]{:S(2)}) copy-start(f32[1,256,256]{2,1,0:T(8,128)} %param.17) | copy-start | bytes 786436
  7.9 34.7 %copy-start.15 = (bf16[1024,1]{0,1:T(2,128)(2,1)S(1)}, bf16[1024,1]{0,1:T(2,128)(2,1)}, u32[]{:S(2)}) copy-start(bf16[1024,1]{0,1:T(2,128)(2,1)} %param.16) | copy-start | bytes 6148
  26.1 16.5 %copy-start.5 = (bf16[1024,256]{1,0:T(8,128)(2,1)S(1)}, bf16[1024,256]{1,0:T(8,128)(2,1)}, u32[]{:S(2)}) copy-start(bf16[1024,256]{1,0:T(8,128)(2,1)} %param.14) | copy-start | bytes 1572868
  26.1 16.5 %copy-start.6 = (bf16[1024,256]{1,0:T(8,128)(2,1)S(1)}, bf16[1024,256]{1,0:T(8,128)(2,1)}, u32[]{:S(2)}) copy-start(bf16[1024,256]{1,0:T(8,128)(2,1)} %param.15) | copy-start | bytes 1572868
  44.4 1.1 copy-start.8
  47.4 1.1 copy-start.10
  49.7 2.5 copy-start.2
  52.1 50.1 %reduce-scatter.9.cloned.1.call-start = ((), (), s32[]{:S(2)}) async-start(), calls=%async_computation.4 | async-start | bytes 1310720 | tf_op jit(solution)/shard_map/reduce_scatter | solution.py:100
  52.9 95.0 %all-gather.7.cloned.1.call-start = ((), (), s32[]{:S(2)}) async-start(), calls=%async_computation.6 | async-start | bytes 1572864 | tf_op jit(solution)/shard_map/all_gather | solution.py:15
  102.2 1.1 copy-start.4
  120.2 57.8 %reduce-scatter.15.cloned.1.call-start = ((), (), s32[]{:S(2)}) async-start(), calls=%async_computation.9 | async-start | bytes 655360
  120.4 0.5 copy-start.16
  149.8 1.1 copy-start.7
  150.8 0.9 copy-start.13
  153.6 2.5 copy-start.3
  156.0 49.6 %reduce-scatter.11.cloned.1.call-start = ((), (), s32[]{:S(2)}) async-start(), calls=%async_computation.5 | async-start | bytes 1310720 | tf_op jit(solution)/shard_map/reduce_scatter | solution.py:100
  156.6 2.1 copy-start.9
  156.6 93.8 %all-gather.9.cloned.1.call-start = ((), (), s32[]{:S(2)}) async-start(), calls=%async_computation.7 | async-start | bytes 1572864 | tf_op jit(solution)/shard_map/all_gather | solution.py:15
  159.1 1.0 copy-start.12
  223.5 0.6 copy-start.17
  250.5 1.5 copy-start.14
  258.4 0.7 copy-start.18
Sparse Core Ops, SparseCore 0:
  52.2 22.0 reduce-scatter.12
  76.6 25.5 reduce-scatter.8
  120.3 24.0 all-gather.6
  156.2 21.7 reduce-scatter.14
  180.1 25.4 reduce-scatter.10
  223.7 23.9 all-gather.8
